TPU v7x, 256 devices: a whole 4x4x8 slice. The times are simulated.
256 devices in a mesh: req: 32 (over z, y), tp: 8 (over x, core).
Axes of the slice: x: 4, y: 4, z: 8, core: 2. Of those that a mesh axis runs over, the one named last changes fastest.
Arguments:
- hidden: bfloat16 [9472, 5120], P('req', 'tp'), may hold values from -6 to 6
- raw_q: bfloat16 [9472, 3072], P('req', 'tp'), may hold values from -70 to 70
- raw_k: bfloat16 [9472, 3072], P('req', 'tp'), may hold values from -70 to 70
- raw_v: bfloat16 [9472, 3072], P('req', 'tp'), may hold values from -6 to 6
- q_gain: float32 [3072], P('tp'), may hold values from 0.5 to 2
- k_gain: float32 [3072], P('tp'), may hold values from 0.5 to 2
- out_weight: bfloat16 [3072, 5120], P('tp'), may hold values from -0.109375 to 0.109375
- post_gain: float32 [5120], P('tp'), may hold values from 0.25 to 1.75
- prefix_keys: bfloat16 [32, 32, 128, 3072], P(None, 'req', None, 'tp'), may hold values from -420 to 420
- prefix_values: bfloat16 [32, 32, 128, 3072], P(None, 'req', None, 'tp'), may hold values from -6 to 6
- key_cache: bfloat16 [256, 128, 3072], P('req', None, 'tp'), may hold values from -420 to 420
- value_cache: bfloat16 [256, 128, 3072], P('req', None, 'tp'), may hold values from -6 to 6
- slot_owner: int32 [256], P('req'), may hold values from -1 to 255, as said below
- slot_page: int32 [256], P('req'), may hold values from 0 to 127, as said below
- cache_lengths: int32 [256], replicated, may hold values from 0 to 16384, as said below
- span_offsets: int32 [32], replicated, may hold values from 0 to 4096
Outputs:
- new_hidden: bfloat16 [9472, 5120], P('req', 'tp')
Inputs may be any that keep to these rules, and one draw needn't show every extreme that they name: Each pool slot holds one page of decode request slot_owner[s], or nothing where it is -1. No page of a request is held twice, and a request holding c pages holds pages 0 to c - 1. `slot_page`: 0 for a slot that holds nothing. `cache_lengths`: A request holding c pages of the pool has a length from (c - 1) * 128 + 1 to c * 128, and 0 where c = 0.
All inputs are finite; a program needn't handle non-finite values.
Results may differ from a plain program's by a relative error of at most 0.0076.
Values may be sent and summed in bfloat16 or wider, within the bound.
A program may use at most 128 MiB of HBM per device.

v0:
```python
import jax
import jax.numpy as jnp
from jax import lax
from jax.sharding import PartitionSpec as P

HD = 128
SPAN = 288
DEC = 8
EPSILON = 1e-06
THETA = 500000.0
NEGATIVE = -1e30


def rotate(values, positions):
    half_width = values.shape[-1] // 2
    frequency = THETA ** (-(jnp.arange(half_width, dtype=jnp.float32) * 2.0 / values.shape[-1]))
    angles = positions.astype(jnp.float32)[:, None] * frequency[None, :]
    cosine = jnp.cos(angles)[:, None, :]
    sine_part = jnp.sin(angles)[:, None, :]
    first_half = values[..., :half_width]
    second = values[..., half_width:]
    return jnp.concatenate(
        [first_half * cosine - second * sine_part, second * cosine + first_half * sine_part], -1
    )


def softmax_part(scores, key_mask, values, form):
    masked = jnp.where(key_mask, scores, NEGATIVE)
    top_score = jnp.max(masked, -1)
    exp_terms = jnp.where(key_mask, jnp.exp(masked - top_score[..., None]), 0.0)
    weight_sum = jnp.sum(exp_terms, -1)
    numerator = jnp.einsum(
        form, exp_terms.astype(jnp.bfloat16), values, preferred_element_type=jnp.float32
    )
    return (top_score, weight_sum, numerator)


def merge_parts(top_scores, weight_sums, numerators):
    best_score = jnp.max(top_scores, 0)
    factor = jnp.exp(top_scores - best_score[None])
    weight_sum = jnp.sum(factor * weight_sums, 0)
    numerator = jnp.sum(factor[..., None] * numerators, 0)
    return numerator / weight_sum[..., None]


def body(
    hidden,
    raw_q,
    raw_k,
    raw_v,
    q_gain,
    k_gain,
    out_weight,
    post_gain,
    prefix_keys,
    prefix_values,
    key_cache,
    value_cache,
    slot_owner,
    slot_page,
    cache_lengths,
    span_offsets,
):
    groups = lax.axis_size("req")
    my_group = lax.axis_index("req")
    tp_count = lax.axis_size("tp")
    rows_group = SPAN + DEC
    local_width = raw_q.shape[1]
    local_heads = local_width // HD
    requests = groups * DEC
    score_scale = HD ** (-0.5)
    page_rows = key_cache.shape[1]
    own_keys = lax.all_to_all(prefix_keys, "req", split_axis=0, concat_axis=1, tiled=True)
    own_values = lax.all_to_all(prefix_values, "req", split_axis=0, concat_axis=1, tiled=True)
    prefix_len = own_keys.shape[1] * page_rows
    own_keys = own_keys.reshape(prefix_len, local_heads, HD)
    own_values = own_values.reshape(prefix_len, local_heads, HD)
    own_lengths = lax.dynamic_slice_in_dim(cache_lengths, my_group * DEC, DEC)
    positions = jnp.concatenate(
        [span_offsets[my_group] + jnp.arange(SPAN, dtype=jnp.int32), own_lengths]
    )
    float_query = raw_q.astype(jnp.float32)
    float_key = raw_k.astype(jnp.float32)
    query_power, key_power = lax.psum(
        (jnp.sum(float_query * float_query, 1), jnp.sum(float_key * float_key, 1)), "tp"
    )
    full_width = local_width * tp_count
    normed_query = (
        float_query * lax.rsqrt(query_power / full_width + EPSILON)[:, None] * q_gain[None, :]
    )
    normed_key = float_key * lax.rsqrt(key_power / full_width + EPSILON)[:, None] * k_gain[None, :]
    query = rotate(normed_query.reshape(rows_group, local_heads, HD), positions).astype(
        jnp.bfloat16
    )
    key_rows = rotate(normed_key.reshape(rows_group, local_heads, HD), positions).astype(
        jnp.bfloat16
    )
    value_rows = raw_v.reshape(rows_group, local_heads, HD)
    decode_queries = lax.all_gather(query[SPAN:], "req", axis=0, tiled=True)
    live_slot = slot_owner >= 0
    owner_index = jnp.maximum(slot_owner, 0)
    slot_queries = decode_queries[owner_index]
    slot_keys = key_cache.reshape(key_cache.shape[0], page_rows, local_heads, HD)
    slot_values = value_cache.reshape(value_cache.shape[0], page_rows, local_heads, HD)
    scores = (
        jnp.einsum("shd,sphd->shp", slot_queries, slot_keys, preferred_element_type=jnp.float32)
        * score_scale
    )
    key_pos = slot_page[:, None] * page_rows + jnp.arange(page_rows, dtype=jnp.int32)[None, :]
    key_mask = live_slot[:, None] & (key_pos < cache_lengths[owner_index][:, None])
    top_score, weight_sum, numerator = softmax_part(
        scores, key_mask[:, None, :], slot_values, "shp,sphd->shd"
    )
    member = slot_owner[None, :] == jnp.arange(requests, dtype=jnp.int32)[:, None]
    best_score = jnp.max(jnp.where(member[:, :, None], top_score[None], NEGATIVE), 1)
    factor = jnp.where(member[:, :, None], jnp.exp(top_score[None] - best_score[:, None]), 0.0)
    request_total = jnp.einsum("rsh,sh->rh", factor, weight_sum, precision=lax.Precision.HIGHEST)
    request_numerator = jnp.einsum(
        "rsh,shd->rhd", factor, numerator, precision=lax.Precision.HIGHEST
    )
    packed = jnp.concatenate(
        [request_numerator, best_score[..., None], request_total[..., None]], -1
    )
    back = lax.all_to_all(packed, "req", split_axis=0, concat_axis=0, tiled=True)
    back = back.reshape(groups, DEC, local_heads, HD + 2)
    own_scores = (
        jnp.sum(query[SPAN:].astype(jnp.float32) * key_rows[SPAN:].astype(jnp.float32), -1)
        * score_scale
    )
    decode_out = merge_parts(
        jnp.concatenate([back[..., HD], own_scores[None]], 0),
        jnp.concatenate([back[..., HD + 1], jnp.ones_like(own_scores)[None]], 0),
        jnp.concatenate([back[..., :HD], value_rows[SPAN:].astype(jnp.float32)[None]], 0),
    )
    span_query = query[:SPAN]
    causal = jnp.arange(SPAN)[:, None] >= jnp.arange(SPAN)[None, :]
    prefix_mask = jnp.arange(prefix_len, dtype=jnp.int32) < span_offsets[my_group]
    pre_scores = (
        jnp.einsum("qhd,khd->qhk", span_query, own_keys, preferred_element_type=jnp.float32)
        * score_scale
    )
    self_scores = (
        jnp.einsum("qhd,khd->qhk", span_query, key_rows[:SPAN], preferred_element_type=jnp.float32)
        * score_scale
    )
    pre_masked = jnp.where(prefix_mask[None, None, :], pre_scores, NEGATIVE)
    self_masked = jnp.where(causal[:, None, :], self_scores, NEGATIVE)
    top = jnp.maximum(jnp.max(pre_masked, -1), jnp.max(self_masked, -1))
    pre_exp = jnp.where(prefix_mask[None, None, :], jnp.exp(pre_masked - top[..., None]), 0.0)
    self_exp = jnp.where(causal[:, None, :], jnp.exp(self_masked - top[..., None]), 0.0)
    total = jnp.sum(pre_exp, -1) + jnp.sum(self_exp, -1)
    span_numerator = jnp.einsum(
        "qhk,khd->qhd", pre_exp.astype(jnp.bfloat16), own_values, preferred_element_type=jnp.float32
    ) + jnp.einsum(
        "qhk,khd->qhd",
        self_exp.astype(jnp.bfloat16),
        value_rows[:SPAN],
        preferred_element_type=jnp.float32,
    )
    span_out = span_numerator / total[..., None]
    merged = jnp.concatenate([span_out, decode_out], 0)
    attention = merged.reshape(rows_group, local_width).astype(jnp.bfloat16)
    share_width = post_gain.shape[0]
    partial = jnp.dot(attention, out_weight, preferred_element_type=jnp.float32)
    my_share = lax.psum_scatter(partial, "tp", scatter_dimension=1, tiled=True)
    power = lax.psum(jnp.sum(my_share * my_share, 1), "tp")
    inverse = lax.rsqrt(power / (share_width * tp_count) + EPSILON)
    normed = my_share * inverse[:, None]
    return (hidden.astype(jnp.float32) + normed * post_gain[None, :]).astype(jnp.bfloat16)


def solution(mesh):
    return jax.shard_map(
        body,
        mesh=mesh,
        in_specs=(
            P("req", "tp"),
            P("req", "tp"),
            P("req", "tp"),
            P("req", "tp"),
            P("tp"),
            P("tp"),
            P("tp", None),
            P("tp"),
            P(None, "req", None, "tp"),
            P(None, "req", None, "tp"),
            P("req", None, "tp"),
            P("req", None, "tp"),
            P("req"),
            P("req"),
            P(),
            P(),
        ),
        out_specs=P("req", "tp"),
        check_vma=False,
    )
```

profile of v0, /device:TPU:8, one launch (start us, length us, event | category | flops | bytes accessed | tf_op | source)
XLA Modules:
  0.0 327.7 jit_solution(14584163546658143109)
XLA Ops:
  8.6 1.6 copy.111
  12.4 14.6 %all-reduce.1 = (f32[296]{0:T(512)S(1)}, f32[296]{0:T(512)S(1)}) all-reduce(f32[296]{0:T(512)S(1)} %fusion.22, f32[296]{0:T(512)S(1)} %fusion.24), channel_id=1, replica_groups=mesh['req'=32,'tp'=8] {'tp'}, use_global_device_ids=true, to_apply=%region_1.0 | all-reduce | flops 592 | bytes 4736 | tf_op jit(solution)/shard_map/psum | solution.py:84
  32.3 1.3 subtract_convert_fusion.1
  34.5 52.2 %all_gather.3 = bf16[256,3,128]{2,0,1:T(8,128)(2,1)S(1)} all-gather(bf16[8,3,128]{2,0,1:T(8,128)(2,1)S(1)} %get-tuple-element.10), channel_id=1, replica_groups=mesh['req'=32,'tp'=8] {'req'}, dimensions={0}, use_global_device_ids=true | all-gather | bytes 202752 | tf_op jit(solution)/shard_map/all_gather | solution.py:99
  89.1 1.5 copy.112
  92.1 1.3 reshape.274
  93.5 21.6 %all_to_all.23 = f32[32,1,3120]{2,1,0:T(1,128)} all-to-all(f32[32,1,3120]{2,1,0:T(1,128)S(1)} %reshape.274), channel_id=1, replica_groups=mesh['req'=32,'tp'=8] {'req'}, dimensions={0} | all-to-all | bytes 798720 | tf_op jit(solution)/shard_map/all_to_all | solution.py:124
  115.1 67.9 %all_to_all.24 = bf16[32,1,128,384]{3,2,1,0:T(8,128)(2,1)} all-to-all(bf16[32,1,128,384]{3,2,1,0:T(8,128)(2,1)} %param.24), channel_id=1, replica_groups=mesh['req'=32,'tp'=8] {'req'}, dimensions={0} | all-to-all | bytes 6291456 | tf_op jit(solution)/shard_map/all_to_all | solution.py:73
  183.0 8.2 %all-to-all-start.1 = ((bf16[32,1,128,384]{3,2,1,0:T(8,128)(2,1)}), bf16[32,1,128,384]{3,2,1,0:T(8,128)(2,1)S(1)}, u32[]{:S(2)}, u32[]{:S(2)}) async-start(bf16[32,1,128,384]{3,2,1,0:T(8,128)(2,1)} %param.25), calls=%async_computation.1 | async-start | bytes 6291456 | tf_op jit(solution)/shard_map/all_to_all | solution.py:74
  191.9 1.3 bitcast_convert_fusion
  193.2 3.3 %fusion.71 = (f32[288,3]{0,1:T(4,128)}, f32[288,3,288]{0,2,1:T(8,128)}) fusion(bf16[296,3,64]{2,0,1:T(8,128)(2,1)S(1)} %get-tuple-element.11, bf16[296,3,64]{2,0,1:T(8,128)(2,1)} %copy-done.2, bf16[296,3,64]{2,0,1:T(8,128)(2,1)} %copy-done.5, bf16[296,3,64]{2,0,1:T(8,128)(2,1)} %copy-done.4, pred[288,288]{0,1:T(8,128)(4,1)S(1)} %iota_compare_fusion), kind=kOutput, calls=%fused_computation.124 | convolution fusion | flops 65331360 | bytes 1536384 | tf_op jit(solution)/shard_map/qhd,khd->qhk/dot_general | solution.py:143
  197.0 3.3 %reduce.3 = f32[32,3120]{1,0:T(8,128)} reduce(f32[32,1,3120]{2,1,0:T(1,128)} %all_to_all.23, f32[]{:T(128)} %broadcast.170), dimensions={1}, to_apply=%all_to_all.8.reduce_sub_computation | reduce | bytes 798724 | tf_op jit(solution)/shard_map/all_to_all | solution.py:124
  200.3 3.3 %reshape.275 = f32[256,3,130]{2,1,0:T(4,128)} reshape(f32[32,3120]{1,0:T(8,128)} %reduce.3) | data formatting | bytes 798720
  203.6 1.4 copy.184
  212.1 9.2 %reshape.272 = bf16[4096,3,128]{2,1,0:T(4,128)(2,1)} reshape(bf16[32,1,128,384]{3,2,1,0:T(8,128)(2,1)} %all_to_all.24) | data formatting | bytes 6291456 | tf_op jit(solution)/shard_map/reshape | solution.py:76
  221.3 9.9 %bitcast_reduce_fusion = (f32[288,3]{0,1:T(4,128)S(1)}, f32[3,288,4096]{2,1,0:T(8,128)}) fusion(pred[4096]{0:T(1024)(128)(4,1)S(1)} %iota_compare_fusion.1, bf16[4096,3,128]{2,1,0:T(4,128)(2,1)} %reshape.272, bf16[296,3,64]{2,0,1:T(8,128)(2,1)S(1)} %get-tuple-element.11, bf16[296,3,64]{2,0,1:T(8,128)(2,1)} %copy-done.2), kind=kOutput, calls=%fused_computation.3 | convolution fusion | flops 917027968 | bytes 17536384 | tf_op jit(solution)/shard_map/qhd,khd->qhk/dot_general | solution.py:139
  231.2 8.9 %fusion.2 = f32[288,3]{0,1:T(4,128)S(1)} fusion(f32[3,288,4096]{2,1,0:T(8,128)} %get-tuple-element.31, f32[288,3]{0,1:T(4,128)S(1)} %max.10, pred[4096]{0:T(1024)(128)(4,1)S(1)} %iota_compare_fusion.1), kind=kLoop, calls=%fused_computation.7 | loop fusion | flops 17693856 | bytes 14166784 | tf_op jit(solution)/shard_map/reduce_sum | solution.py:151
  240.1 6.7 %all-to-all-done.1 = bf16[32,1,128,384]{3,2,1,0:T(8,128)(2,1)S(1)} async-done(((bf16[32,1,128,384]{3,2,1,0:T(8,128)(2,1)}), bf16[32,1,128,384]{3,2,1,0:T(8,128)(2,1)S(1)}, u32[]{:S(2)}, u32[]{:S(2)}) %all-to-all-start.1) | async-done | bytes 3145760 | tf_op jit(solution)/shard_map/all_to_all | solution.py:74
  246.8 3.9 %reshape.273 = bf16[4096,3,128]{2,1,0:T(4,128)(2,1)} reshape(bf16[32,1,128,384]{3,2,1,0:T(8,128)(2,1)S(1)} %all-to-all-done.1) | data formatting | bytes 6291456 | tf_op jit(solution)/shard_map/reshape | solution.py:77
  250.6 8.6 %fusion.4 = f32[3,288,128]{2,1,0:T(8,128)S(1)} fusion(f32[3,288,4096]{2,1,0:T(8,128)} %get-tuple-element.31, f32[288,3]{0,1:T(4,128)S(1)} %max.10, pred[4096]{0:T(1024)(128)(4,1)S(1)} %iota_compare_fusion.1, bf16[4096,3,128]{2,1,0:T(4,128)(2,1)} %reshape.273), kind=kOutput, calls=%fused_computation.9 | convolution fusion | flops 923664384 | bytes 17751424 | tf_op jit(solution)/shard_map/qhk,khd->qhd/dot_general | solution.py:152
  261.3 4.4 %fusion.27 = f32[296,5120]{1,0:T(8,128)} fusion(bf16[384,5120]{1,0:T(8,128)(2,1)S(1)} %copy-done.1, bf16[8,3,128]{2,0,1:T(8,128)(2,1)S(1)} %divide_convert_fusion, bf16[288,3,128]{2,0,1:T(8,128)(2,1)S(1)} %fusion.15), kind=kOutput, calls=%fused_computation.48 | convolution fusion | flops 1164374016 | bytes 10221568 | tf_op jit(solution)/shard_map/dot_general | solution.py:164
  265.7 37.9 %reduce-scatter.2.cloned.1.call-done = f32[296,640]{1,0:T(8,128)} async-done(((f32[296,5120]{1,0:T(8,128)}), f32[296,640]{1,0:T(8,128)}) %reduce-scatter.2.cloned.1.call-update) | async-done | bytes 757776 | tf_op jit(solution)/shard_map/reduce_scatter | solution.py:165
  304.9 13.9 %psum.23 = f32[296]{0:T(512)S(1)} all-reduce(f32[296]{0:T(512)S(1)} %multiply_reduce_fusion), channel_id=1, replica_groups=mesh['req'=32,'tp'=8] {'tp'}, use_global_device_ids=true, to_apply=%region_17.18 | all-reduce | flops 296 | bytes 2368 | tf_op jit(solution)/shard_map/psum | solution.py:166
  318.8 2.1 add_convert_fusion
  (86 shorter events, 25.8 us)
Async XLA Ops:
  6.5 23.4 %copy-start.6 = (bf16[296,384]{1,0:T(8,128)(2,1)S(1)}, bf16[296,384]{1,0:T(8,128)(2,1)}, u32[]{:S(2)}) copy-start(bf16[296,384]{1,0:T(8,128)(2,1)} %param.18) | copy-start | bytes 681988
  6.5 22.2 %copy-start.12 = (s32[32]{0:T(128)S(1)}, s32[32]{0:T(128)}, u32[]{:S(2)}) copy-start(s32[32]{0:T(128)} %param.31) | copy-start | bytes 388
  6.5 23.5 %copy-start.10 = (f32[384]{0:T(512)S(1)}, f32[384]{0:T(512)}, u32[]{:S(2)}) copy-start(f32[384]{0:T(512)} %param.21) | copy-start | bytes 4612
  12.4 19.1 %copy-start = (s32[256]{0:T(256)S(1)}, s32[256]{0:T(256)}, u32[]{:S(2)}) copy-start(s32[256]{0:T(256)} %param.30) | copy-start | bytes 3076
  30.3 57.8 %copy-start.13 = (s32[8]{0:T(128)S(1)}, s32[8]{0:T(128)}, u32[]{:S(2)}) copy-start(s32[8]{0:T(128)} %param.29) | copy-start | bytes 100
  33.6 0.7 copy-start.5
  33.6 55.5 %copy-start.2 = (bf16[296,3,64]{2,0,1:T(8,128)(2,1)}, bf16[296,3,64]{2,0,1:T(8,128)(2,1)S(1)}, u32[]{:S(2)}) copy-start(bf16[296,3,64]{2,0,1:T(8,128)(2,1)S(1)} %get-tuple-element.12) | copy-start | bytes 340996
  33.6 55.5 %copy-start.4 = (bf16[296,3,64]{2,0,1:T(8,128)(2,1)}, bf16[296,3,64]{2,0,1:T(8,128)(2,1)S(1)}, u32[]{:S(2)}) copy-start(bf16[296,3,64]{2,0,1:T(8,128)(2,1)S(1)} %get-tuple-element.22) | copy-start | bytes 340996
  183.0 63.8 %all-to-all-start.1 = ((bf16[32,1,128,384]{3,2,1,0:T(8,128)(2,1)}), bf16[32,1,128,384]{3,2,1,0:T(8,128)(2,1)S(1)}, u32[]{:S(2)}, u32[]{:S(2)}) async-start(bf16[32,1,128,384]{3,2,1,0:T(8,128)(2,1)} %param.25), calls=%async_computation.1 | async-start | bytes 6291456 | tf_op jit(solution)/shard_map/all_to_all | solution.py:74
  191.2 112.4 %reduce-scatter.2.cloned.1.call-start = ((), (), s32[]{:S(2)}) async-start(), calls=%async_computation.4 | async-start | bytes 6819840 | tf_op jit(solution)/shard_map/reduce_scatter | solution.py:165
  221.3 9.9 %copy-start.8 = (f32[288,3]{0,1:T(4,128)S(1)}, f32[288,3]{0,1:T(4,128)}, u32[]{:S(2)}) copy-start(f32[288,3]{0,1:T(4,128)} %get-tuple-element.32) | copy-start | bytes 10372
  250.6 8.6 %copy-start.3 = (f32[288,3,288]{0,2,1:T(8,128)S(1)}, f32[288,3,288]{0,2,1:T(8,128)}, u32[]{:S(2)}) copy-start(f32[288,3,288]{0,2,1:T(8,128)} %get-tuple-element.33) | copy-start | bytes 2985988
  250.6 8.9 %copy-start.11 = (bf16[296,384]{1,0:T(8,128)(2,1)S(1)}, bf16[296,384]{1,0:T(8,128)(2,1)}, u32[]{:S(2)}) copy-start(bf16[296,384]{1,0:T(8,128)(2,1)} %param.19) | copy-start | bytes 681988
  259.2 2.1 copy-start.1
  265.7 53.1 %copy-start.7 = (bf16[296,640]{1,0:T(8,128)(2,1)S(1)}, bf16[296,640]{1,0:T(8,128)(2,1)}, u32[]{:S(2)}) copy-start(bf16[296,640]{1,0:T(8,128)(2,1)} %param.16) | copy-start | bytes 1136644
  265.7 53.1 %copy-start.9 = (f32[640]{0:T(1024)S(1)}, f32[640]{0:T(1024)}, u32[]{:S(2)}) copy-start(f32[640]{0:T(1024)} %param.23) | copy-start | bytes 7684
Sparse Core Ops, SparseCore 0:
  265.8 37.7 reduce-scatter.1
where the time goes:
time: 329 us; the launch traced here: 328 us
  blocking collectives  170 us (52%)
  waiting for transfers between devices  44.6 us (14%)
  local copies, waits for them, and re-layouts  33.2 us (10%)
  other arithmetic  29.4 us (9%)
  matrix products  28.3 us (9%)
  between operations  13.7 us (4%)
  starting transfers between devices  8.25 us (3%)
    all_to_all x1, blocking collectives, body(): lax.all_to_all(prefix_keys, 'req', split_axis=0, concat_axis=1, tiled=True)  67.9 us
    all_gather x1, blocking collectives, body(): decode_queries = lax.all_gather(query[SPAN:], 'req', axis=0, tiled=True)  52.2 us
    reduce_scatter x1, waiting for transfers between devices, body(): my_share = lax.psum_scatter(partial, 'tp', scatter_dimension=1, tiled=True)  37.9 us
    all_to_all x1, blocking collectives, body(): lax.all_to_all(packed, 'req', split_axis=0, concat_axis=0, tiled=True)  21.6 us
    psum x1, blocking collectives, body(): lax.psum((jnp.sum(float_query * float_query, 1), jnp.sum(float_key * floa...  14.6 us
    psum x1, blocking collectives, body(): power = lax.psum(jnp.sum(my_share * my_share, 1), 'tp')  13.9 us
    dot_general x1, matrix products, body(): jnp.einsum('qhd,khd->qhk', span_query, own_keys, preferred_element_type=j...  9.93 us
    unnamed x32, local copies, waits for them, and re-layouts  9.72 us
  transfers between devices with their start and end apart: 2, of which 2 were waited for; matrix products, arithmetic and copies ran while one was open for 15% of the time, Pallas kernels for 0%

commit v1 on v0

--- a/solution.py
+++ b/solution.py
@@ -96,7 +96,9 @@
         jnp.bfloat16
     )
     value_rows = raw_v.reshape(rows_group, local_heads, HD)
-    decode_queries = lax.all_gather(query[SPAN:], "req", axis=0, tiled=True)
+    decode_queries = jnp.concatenate(
+        lax.all_to_all(jnp.stack([query[SPAN:]] * lax.axis_size("req")), "req", 0, 0), axis=0
+    )
     live_slot = slot_owner >= 0
     owner_index = jnp.maximum(slot_owner, 0)
     slot_queries = decode_queries[owner_index]

time: 329 us -> 313 us (0.951)
  blocking collectives: 170 us -> 120 us
  waiting for transfers between devices: 44.6 us -> 72.6 us
  starting transfers between devices: 8.25 us -> 17.3 us
    all_gather x1 -> x0, blocking collectives: 52.2 us -> none  [body(): decode_queries = lax.all_gather(query[SPAN:], 'req', axis=0, tiled=True)]
    all_to_all x1, waiting for transfers between devices: 6.65 us -> 19.1 us  [body(): lax.all_to_all(prefix_values, 'req', split_axis=0, concat_axis=1, tiled=T...]
    all_to_all x0 -> x1, starting transfers between devices: none -> 11.7 us  [body(): lax.all_to_all(jnp.stack([query[SPAN:]] * lax.axis_size('req')), 'req', 0...]
    reduce_scatter x1, waiting for transfers between devices: 37.9 us -> 48.1 us  [body(): my_share = lax.psum_scatter(partial, 'tp', scatter_dimension=1, tiled=True)]
    all_to_all x1, blocking collectives: 67.9 us -> 75 us  [body(): lax.all_to_all(prefix_keys, 'req', split_axis=0, concat_axis=1, tiled=True)]
    all_to_all x0 -> x1, waiting for transfers between devices: none -> 5.31 us  [body(): lax.all_to_all(jnp.stack([query[SPAN:]] * lax.axis_size('req')), 'req', 0...]
    all_to_all x1, blocking collectives: 21.6 us -> 16.8 us  [body(): lax.all_to_all(packed, 'req', split_axis=0, concat_axis=0, tiled=True)]
    unnamed x32 -> x34, local copies, waits for them, and re-layouts: 9.72 us -> 9.65 us
  transfers between devices with their start and end apart: 2 -> 3, of which waited for: 2 -> 3; matrix products, arithmetic and copies ran while one was open for 15% -> 17% of each run, Pallas kernels for 0% -> 0%
where the time goes in v1:
time: 313 us; the launch traced here: 312 us
  blocking collectives  120 us (38%)
  waiting for transfers between devices  72.6 us (23%)
  local copies, waits for them, and re-layouts  33.1 us (11%)
  matrix products  28.3 us (9%)
  other arithmetic  26.4 us (8%)
  starting transfers between devices  17.3 us (6%)
  between operations  13.8 us (4%)
    all_to_all x1, blocking collectives, body(): lax.all_to_all(prefix_keys, 'req', split_axis=0, concat_axis=1, tiled=True)  75 us
    reduce_scatter x1, waiting for transfers between devices, body(): my_share = lax.psum_scatter(partial, 'tp', scatter_dimension=1, tiled=True)  48.1 us
    all_to_all x1, waiting for transfers between devices, body(): lax.all_to_all(prefix_values, 'req', split_axis=0, concat_axis=1, tiled=T...  19.1 us
    all_to_all x1, blocking collectives, body(): lax.all_to_all(packed, 'req', split_axis=0, concat_axis=0, tiled=True)  16.8 us
    psum x1, blocking collectives, body(): lax.psum((jnp.sum(float_query * float_query, 1), jnp.sum(float_key * floa...  14.6 us
    psum x1, blocking collectives, body(): power = lax.psum(jnp.sum(my_share * my_share, 1), 'tp')  13.9 us
    all_to_all x1, starting transfers between devices, body(): lax.all_to_all(jnp.stack([query[SPAN:]] * lax.axis_size('req')), 'req', 0...  11.7 us
    dot_general x1, matrix products, body(): jnp.einsum('qhd,khd->qhk', span_query, own_keys, preferred_element_type=j...  9.93 us
  transfers between devices with their start and end apart: 3, of which 3 were waited for; matrix products, arithmetic and copies ran while one was open for 17% of the time, Pallas kernels for 0%

profile of v1, /device:TPU:8, one launch (start us, length us, event | category | flops | bytes accessed | tf_op | source)
XLA Modules:
  0.0 311.8 jit_solution(12591946263039529448)
XLA Ops:
  8.8 14.6 %all-reduce.1 = (f32[296]{0:T(512)S(1)}, f32[296]{0:T(512)S(1)}) all-reduce(f32[296]{0:T(512)S(1)} %fusion.22, f32[296]{0:T(512)S(1)} %fusion.24), channel_id=1, replica_groups=mesh['req'=32,'tp'=8] {'tp'}, use_global_device_ids=true, to_apply=%region_1.0 | all-reduce | flops 592 | bytes 4736 | tf_op jit(solution)/shard_map/psum | solution.py:84
  29.7 11.7 %all-to-all-start.2 = ((bf16[32,8,3,128]{3,1,2,0:T(8,128)(2,1)}), bf16[32,8,3,128]{3,1,2,0:T(8,128)(2,1)S(1)}, u32[]{:S(2)}, u32[]{:S(2)}) async-start(bf16[32,8,3,128]{3,1,2,0:T(8,128)(2,1)} %stack.2), calls=%async_computation.2 | async-start | bytes 393216 | tf_op jit(solution)/shard_map/all_to_all | solution.py:100
  41.5 1.5 copy.155
  43.7 1.5 copy.156
  45.3 5.3 %all-to-all-done.2 = bf16[32,8,3,128]{3,1,2,0:T(8,128)(2,1)S(1)} async-done(((bf16[32,8,3,128]{3,1,2,0:T(8,128)(2,1)}), bf16[32,8,3,128]{3,1,2,0:T(8,128)(2,1)S(1)}, u32[]{:S(2)}, u32[]{:S(2)}) %all-to-all-start.2) | async-done | bytes 196640 | tf_op jit(solution)/shard_map/all_to_all | solution.py:100
  53.9 1.3 reshape.280
  55.2 16.8 %all_to_all.28 = f32[32,1,3120]{2,1,0:T(1,128)} all-to-all(f32[32,1,3120]{2,1,0:T(1,128)S(1)} %reshape.280), channel_id=1, replica_groups=mesh['req'=32,'tp'=8] {'req'}, dimensions={0} | all-to-all | bytes 798720 | tf_op jit(solution)/shard_map/all_to_all | solution.py:126
  72.0 75.0 %all_to_all.29 = bf16[32,1,128,384]{3,2,1,0:T(8,128)(2,1)} all-to-all(bf16[32,1,128,384]{3,2,1,0:T(8,128)(2,1)} %param.24), channel_id=1, replica_groups=mesh['req'=32,'tp'=8] {'req'}, dimensions={0} | all-to-all | bytes 6291456 | tf_op jit(solution)/shard_map/all_to_all | solution.py:73
  147.0 5.6 %all-to-all-start.1 = ((bf16[32,1,128,384]{3,2,1,0:T(8,128)(2,1)}), bf16[32,1,128,384]{3,2,1,0:T(8,128)(2,1)S(1)}, u32[]{:S(2)}, u32[]{:S(2)}) async-start(bf16[32,1,128,384]{3,2,1,0:T(8,128)(2,1)} %param.25), calls=%async_computation.1 | async-start | bytes 6291456 | tf_op jit(solution)/shard_map/all_to_all | solution.py:74
  153.3 1.3 bitcast_convert_fusion
  154.6 3.3 %fusion.71 = (f32[288,3]{0,1:T(4,128)}, f32[288,3,288]{0,2,1:T(8,128)}) fusion(bf16[296,3,64]{2,0,1:T(8,128)(2,1)S(1)} %get-tuple-element.11, bf16[296,3,64]{2,0,1:T(8,128)(2,1)} %copy-done.2, bf16[296,3,64]{2,0,1:T(8,128)(2,1)} %copy-done.5, bf16[296,3,64]{2,0,1:T(8,128)(2,1)} %copy-done.4, pred[288,288]{0,1:T(8,128)(4,1)S(1)} %iota_compare_fusion), kind=kOutput, calls=%fused_computation.125 | convolution fusion | flops 65331360 | bytes 1536384 | tf_op jit(solution)/shard_map/qhd,khd->qhk/dot_general | solution.py:145
  158.4 3.3 %reduce.3 = f32[32,3120]{1,0:T(8,128)} reduce(f32[32,1,3120]{2,1,0:T(1,128)} %all_to_all.28, f32[]{:T(128)} %broadcast.172), dimensions={1}, to_apply=%all_to_all.11.reduce_sub_computation | reduce | bytes 798724 | tf_op jit(solution)/shard_map/all_to_all | solution.py:126
  161.7 3.3 %reshape.281 = f32[256,3,130]{2,1,0:T(4,128)} reshape(f32[32,3120]{1,0:T(8,128)} %reduce.3) | data formatting | bytes 798720
  165.0 1.4 copy.229
  173.5 9.2 %reshape.278 = bf16[4096,3,128]{2,1,0:T(4,128)(2,1)} reshape(bf16[32,1,128,384]{3,2,1,0:T(8,128)(2,1)} %all_to_all.29) | data formatting | bytes 6291456 | tf_op jit(solution)/shard_map/reshape | solution.py:76
  182.7 9.9 %bitcast_reduce_fusion = (f32[288,3]{0,1:T(4,128)S(1)}, f32[3,288,4096]{2,1,0:T(8,128)}) fusion(pred[4096]{0:T(1024)(128)(4,1)S(1)} %iota_compare_fusion.1, bf16[4096,3,128]{2,1,0:T(4,128)(2,1)} %reshape.278, bf16[296,3,64]{2,0,1:T(8,128)(2,1)S(1)} %get-tuple-element.11, bf16[296,3,64]{2,0,1:T(8,128)(2,1)} %copy-done.2), kind=kOutput, calls=%fused_computation.3 | convolution fusion | flops 917027968 | bytes 17536384 | tf_op jit(solution)/shard_map/qhd,khd->qhk/dot_general | solution.py:141
  192.6 8.9 %fusion.2 = f32[288,3]{0,1:T(4,128)S(1)} fusion(f32[3,288,4096]{2,1,0:T(8,128)} %get-tuple-element.31, f32[288,3]{0,1:T(4,128)S(1)} %max.10, pred[4096]{0:T(1024)(128)(4,1)S(1)} %iota_compare_fusion.1), kind=kLoop, calls=%fused_computation.7 | loop fusion | flops 17693856 | bytes 14166784 | tf_op jit(solution)/shard_map/reduce_sum | solution.py:153
  201.5 19.1 %all-to-all-done.1 = bf16[32,1,128,384]{3,2,1,0:T(8,128)(2,1)S(1)} async-done(((bf16[32,1,128,384]{3,2,1,0:T(8,128)(2,1)}), bf16[32,1,128,384]{3,2,1,0:T(8,128)(2,1)S(1)}, u32[]{:S(2)}, u32[]{:S(2)}) %all-to-all-start.1) | async-done | bytes 3145760 | tf_op jit(solution)/shard_map/all_to_all | solution.py:74
  220.6 3.9 %reshape.279 = bf16[4096,3,128]{2,1,0:T(4,128)(2,1)} reshape(bf16[32,1,128,384]{3,2,1,0:T(8,128)(2,1)S(1)} %all-to-all-done.1) | data formatting | bytes 6291456 | tf_op jit(solution)/shard_map/reshape | solution.py:77
  224.5 8.6 %fusion.4 = f32[3,288,128]{2,1,0:T(8,128)S(1)} fusion(f32[3,288,4096]{2,1,0:T(8,128)} %get-tuple-element.31, f32[288,3]{0,1:T(4,128)S(1)} %max.10, pred[4096]{0:T(1024)(128)(4,1)S(1)} %iota_compare_fusion.1, bf16[4096,3,128]{2,1,0:T(4,128)(2,1)} %reshape.279), kind=kOutput, calls=%fused_computation.9 | convolution fusion | flops 923664384 | bytes 17751424 | tf_op jit(solution)/shard_map/qhk,khd->qhd/dot_general | solution.py:154
  235.2 4.4 %fusion.27 = f32[296,5120]{1,0:T(8,128)} fusion(bf16[384,5120]{1,0:T(8,128)(2,1)S(1)} %copy-done.1, bf16[8,3,128]{2,0,1:T(8,128)(2,1)S(1)} %divide_convert_fusion, bf16[288,3,128]{2,0,1:T(8,128)(2,1)S(1)} %fusion.15), kind=kOutput, calls=%fused_computation.48 | convolution fusion | flops 1164374016 | bytes 10221568 | tf_op jit(solution)/shard_map/dot_general | solution.py:166
  239.6 48.1 %reduce-scatter.2.cloned.1.call-done = f32[296,640]{1,0:T(8,128)} async-done(((f32[296,5120]{1,0:T(8,128)}), f32[296,640]{1,0:T(8,128)}) %reduce-scatter.2.cloned.1.call-update) | async-done | bytes 757776 | tf_op jit(solution)/shard_map/reduce_scatter | solution.py:167
  289.0 13.9 %psum.23 = f32[296]{0:T(512)S(1)} all-reduce(f32[296]{0:T(512)S(1)} %multiply_reduce_fusion), channel_id=1, replica_groups=mesh['req'=32,'tp'=8] {'tp'}, use_global_device_ids=true, to_apply=%region_17.18 | all-reduce | flops 296 | bytes 2368 | tf_op jit(solution)/shard_map/psum | solution.py:168
  302.9 2.1 add_convert_fusion
  (91 shorter events, 24.0 us)
Async XLA Ops:
  6.5 19.8 %copy-start.6 = (bf16[296,384]{1,0:T(8,128)(2,1)S(1)}, bf16[296,384]{1,0:T(8,128)(2,1)}, u32[]{:S(2)}) copy-start(bf16[296,384]{1,0:T(8,128)(2,1)} %param.18) | copy-start | bytes 681988
  6.5 18.5 %copy-start.13 = (s32[32]{0:T(128)S(1)}, s32[32]{0:T(128)}, u32[]{:S(2)}) copy-start(s32[32]{0:T(128)} %param.31) | copy-start | bytes 388
  6.5 19.8 %copy-start.10 = (f32[384]{0:T(512)S(1)}, f32[384]{0:T(512)}, u32[]{:S(2)}) copy-start(f32[384]{0:T(512)} %param.21) | copy-start | bytes 4612
  8.8 18.3 %copy-start = (s32[256]{0:T(256)S(1)}, s32[256]{0:T(256)}, u32[]{:S(2)}) copy-start(s32[256]{0:T(256)} %param.30) | copy-start | bytes 3076
  26.7 14.7 %copy-start.11 = (s32[8]{0:T(128)S(1)}, s32[8]{0:T(128)}, u32[]{:S(2)}) copy-start(s32[8]{0:T(128)} %param.28) | copy-start | bytes 100
  27.9 17.3 %copy-start.14 = (s32[8]{0:T(128)S(1)}, s32[8]{0:T(128)}, u32[]{:S(2)}) copy-start(s32[8]{0:T(128)} %param.29) | copy-start | bytes 100
  28.1 0.7 copy-start.5
  28.1 14.9 %copy-start.2 = (bf16[296,3,64]{2,0,1:T(8,128)(2,1)}, bf16[296,3,64]{2,0,1:T(8,128)(2,1)S(1)}, u32[]{:S(2)}) copy-start(bf16[296,3,64]{2,0,1:T(8,128)(2,1)S(1)} %get-tuple-element.12) | copy-start | bytes 340996
  28.2 14.9 %copy-start.4 = (bf16[296,3,64]{2,0,1:T(8,128)(2,1)}, bf16[296,3,64]{2,0,1:T(8,128)(2,1)S(1)}, u32[]{:S(2)}) copy-start(bf16[296,3,64]{2,0,1:T(8,128)(2,1)S(1)} %get-tuple-element.22) | copy-start | bytes 340996
  29.7 20.9 %all-to-all-start.2 = ((bf16[32,8,3,128]{3,1,2,0:T(8,128)(2,1)}), bf16[32,8,3,128]{3,1,2,0:T(8,128)(2,1)S(1)}, u32[]{:S(2)}, u32[]{:S(2)}) async-start(bf16[32,8,3,128]{3,1,2,0:T(8,128)(2,1)} %stack.2), calls=%async_computation.2 | async-start | bytes 393216 | tf_op jit(solution)/shard_map/all_to_all | solution.py:100
  147.0 73.6 %all-to-all-start.1 = ((bf16[32,1,128,384]{3,2,1,0:T(8,128)(2,1)}), bf16[32,1,128,384]{3,2,1,0:T(8,128)(2,1)S(1)}, u32[]{:S(2)}, u32[]{:S(2)}) async-start(bf16[32,1,128,384]{3,2,1,0:T(8,128)(2,1)} %param.25), calls=%async_computation.1 | async-start | bytes 6291456 | tf_op jit(solution)/shard_map/all_to_all | solution.py:74
  152.6 135.1 %reduce-scatter.2.cloned.1.call-start = ((), (), s32[]{:S(2)}) async-start(), calls=%async_computation.5 | async-start | bytes 6819840 | tf_op jit(solution)/shard_map/reduce_scatter | solution.py:167
  182.7 9.9 %copy-start.8 = (f32[288,3]{0,1:T(4,128)S(1)}, f32[288,3]{0,1:T(4,128)}, u32[]{:S(2)}) copy-start(f32[288,3]{0,1:T(4,128)} %get-tuple-element.32) | copy-start | bytes 10372
  224.5 8.6 %copy-start.3 = (f32[288,3,288]{0,2,1:T(8,128)S(1)}, f32[288,3,288]{0,2,1:T(8,128)}, u32[]{:S(2)}) copy-start(f32[288,3,288]{0,2,1:T(8,128)} %get-tuple-element.33) | copy-start | bytes 2985988
  224.5 8.9 %copy-start.12 = (bf16[296,384]{1,0:T(8,128)(2,1)S(1)}, bf16[296,384]{1,0:T(8,128)(2,1)}, u32[]{:S(2)}) copy-start(bf16[296,384]{1,0:T(8,128)(2,1)} %param.19) | copy-start | bytes 681988
  233.0 2.1 copy-start.1
  239.5 63.3 %copy-start.7 = (bf16[296,640]{1,0:T(8,128)(2,1)S(1)}, bf16[296,640]{1,0:T(8,128)(2,1)}, u32[]{:S(2)}) copy-start(bf16[296,640]{1,0:T(8,128)(2,1)} %param.16) | copy-start | bytes 1136644
  239.5 63.4 %copy-start.9 = (f32[640]{0:T(1024)S(1)}, f32[640]{0:T(1024)}, u32[]{:S(2)}) copy-start(f32[640]{0:T(1024)} %param.23) | copy-start | bytes 7684
Sparse Core Ops, SparseCore 0:
  239.7 47.9 reduce-scatter.1
